TPU v7x, 32 devices: a whole 2x2x4 slice. The times are simulated.
32 devices in a mesh: context: 4 (over z), tensor: 2 (over core), dp: 4 (over y, x).
Axes of the slice: x: 2, y: 2, z: 4, core: 2. Of those that a mesh axis runs over, the one named last changes fastest.
Arguments:
- queries: bfloat16 [4, 3072, 2048], P('dp', 'context', 'tensor'), may hold values from -1.75 to 1.75
- keys_in: bfloat16 [4, 3072, 2048], P('dp', 'context', 'tensor'), may hold values from -1.75 to 1.75
- values: bfloat16 [4, 3072, 2048], P('dp', 'context', 'tensor'), may hold values from -48 to 48
- norm_gain: float32 [2048], P('tensor'), may hold values from 0.25 to 1.75
- segment_ids: int32 [4, 48], P('dp', 'context'), may hold values from 0 to 5, never falling along the last dimension, each value on 1 to 24 neighbouring positions
- grad_out: bfloat16 [4, 3072, 2048], P('dp', 'context', 'tensor'), may hold values from -8 to 8
Outputs:
- normed_out: bfloat16 [4, 3072, 2048], P('dp', 'context', 'tensor')
- grad_queries: bfloat16 [4, 3072, 2048], P('dp', 'context', 'tensor')
- grad_keys: bfloat16 [4, 3072, 2048], P('dp', 'context', 'tensor')
- grad_values: bfloat16 [4, 3072, 2048], P('dp', 'context', 'tensor')
- grad_gain: float32 [2048], P('tensor')
Inputs may be any that keep to these rules, and one draw needn't show every extreme that they name: `segment_ids`: along each sequence the ids never fall; each id is one document.
All inputs are finite; a program needn't handle non-finite values.
Results may differ from a plain program's by a relative error of at most 0.0057.
Values sent between devices are 32-bit elements; how exact they have to be, the bound alone decides.
A program may use at most 128 MiB of HBM per device.

v0:
```python
import jax
import jax.numpy as jnp
from jax import lax
from jax.sharding import PartitionSpec as P

HD = 128
BLK = 256
SEGB = 64
WIDTH = 2048


def shifted(block, axis, distance):
    devices = range(lax.axis_size(axis))
    route = [(i - distance, i) for i in devices if i - distance in devices]
    return lax.ppermute(block, axis, route)


def prefix(value, axis, combine, identity):
    size, place = (lax.axis_size(axis), lax.axis_index(axis))
    everything = jax.tree.map(lambda part: lax.all_gather(part, axis), value)
    start = jax.tree.map(
        lambda part, zero: jnp.broadcast_to(jnp.asarray(zero, part.dtype), part.shape),
        value,
        identity,
    )

    def step(k, before):
        at = size - 1 - k
        reached = at > place
        new = combine(before, jax.tree.map(lambda part: part[at], everything))
        return jax.tree.map(lambda a, b: jnp.where(reached, a, b), new, before)

    return lax.fori_loop(0, size, step, start)


def join_forward(earlier, later):
    early_state, early_segs = earlier
    late_state, late_segs = later
    matches = jnp.logical_or(
        jnp.logical_and(early_segs[1] == late_segs[0], late_segs[0] == late_segs[1]),
        late_segs[0] == 0.0,
    )
    joined = late_state + jnp.where(matches, early_state, 0.0)
    first_seg = jnp.where(early_segs[0] == 0.0, late_segs[0], early_segs[0])
    last_seg = jnp.where(late_segs[1] == 0.0, early_segs[1], late_segs[1])
    return (joined, jnp.stack([first_seg, last_seg]))


def join_backward(earlier, later):
    high_state, high_segs = earlier
    low_state, low_segs = later
    matches = jnp.logical_or(
        jnp.logical_and(high_segs[0] == low_segs[1], low_segs[0] == low_segs[1]), low_segs[0] == 0.0
    )
    joined = low_state + jnp.where(matches, high_state, 0.0)
    first_seg = jnp.where(low_segs[0] == 0.0, high_segs[0], low_segs[0])
    last_seg = jnp.where(high_segs[1] == 0.0, low_segs[1], high_segs[1])
    return (joined, jnp.stack([first_seg, last_seg]))


def block_mask(seg_block):
    length = seg_block.shape[0]
    row_index = lax.broadcasted_iota(jnp.int32, (length, length), 0)
    col_index = lax.broadcasted_iota(jnp.int32, (length, length), 1)
    return jnp.logical_and(row_index >= col_index, seg_block[:, None] == seg_block[None, :])


def forward_block(carried, block_in):
    kv_state, seg_prev = carried
    q_block, k_block, v_block, seg_block = block_in
    visible = block_mask(seg_block)
    scores = jnp.einsum("thd,shd->hts", q_block, k_block, preferred_element_type=jnp.float32)
    weights = jnp.where(visible[None], scores, 0.0).astype(jnp.bfloat16)
    intra = jnp.einsum("hts,she->the", weights, v_block, preferred_element_type=jnp.float32)
    state_bf = kv_state.astype(jnp.bfloat16)
    inter = jnp.einsum("thd,hde->the", q_block, state_bf, preferred_element_type=jnp.float32)
    matches = (seg_block == seg_prev)[:, None, None]
    attended = intra + jnp.where(matches, inter, 0.0)
    last_seg = seg_block[-1]
    in_last = (seg_block == last_seg)[:, None, None]
    added = jnp.einsum(
        "thd,the->hde",
        jnp.where(in_last, k_block, jnp.zeros_like(k_block)),
        v_block,
        preferred_element_type=jnp.float32,
    )
    new_state = jnp.where(seg_prev == last_seg, kv_state, 0.0) + added
    return ((new_state, last_seg), (attended, weights, state_bf, seg_prev))


def backward_block(grad_state, block_in):
    q_block, k_block, v_block, seg_block, grad_block, weights, state_bf, seg_prev = block_in
    visible = block_mask(seg_block)
    grad_scores = jnp.einsum(
        "the,she->hts", grad_block, v_block, preferred_element_type=jnp.float32
    )
    grad_weights = jnp.where(visible[None], grad_scores, 0.0).astype(jnp.bfloat16)
    grad_bf = grad_state.astype(jnp.bfloat16)
    before = (seg_block == seg_prev)[:, None, None]
    after = (seg_block == seg_block[-1])[:, None, None]
    grad_q = jnp.einsum("hts,shd->thd", grad_weights, k_block, preferred_element_type=jnp.float32)
    grad_q = grad_q + jnp.where(
        before,
        jnp.einsum("the,hde->thd", grad_block, state_bf, preferred_element_type=jnp.float32),
        0.0,
    )
    grad_k = jnp.einsum("hts,thd->shd", grad_weights, q_block, preferred_element_type=jnp.float32)
    grad_k = grad_k + jnp.where(
        after, jnp.einsum("she,hde->shd", v_block, grad_bf, preferred_element_type=jnp.float32), 0.0
    )
    grad_v = jnp.einsum("hts,the->she", weights, grad_block, preferred_element_type=jnp.float32)
    grad_v = grad_v + jnp.where(
        after, jnp.einsum("shd,hde->she", k_block, grad_bf, preferred_element_type=jnp.float32), 0.0
    )
    added = jnp.einsum(
        "thd,the->hde",
        jnp.where(before, q_block, jnp.zeros_like(q_block)),
        grad_block,
        preferred_element_type=jnp.float32,
    )
    new_grad = jnp.where(seg_prev == seg_block[-1], grad_state, 0.0) + added
    return (
        new_grad,
        (grad_q.astype(jnp.bfloat16), grad_k.astype(jnp.bfloat16), grad_v.astype(jnp.bfloat16)),
    )


def body(queries, keys_in, values, norm_gain, segment_ids, grad_out):
    tok_count = queries.shape[1]
    local_width = queries.shape[2]
    head_count = local_width // HD
    block_count = tok_count // BLK
    seg_tok = jnp.repeat(segment_ids[0], SEGB)
    seg_blocks = seg_tok.reshape(block_count, BLK)
    flat_q = queries[0].reshape(tok_count, head_count, HD)
    flat_k = keys_in[0].reshape(tok_count, head_count, HD)
    flat_v = values[0].reshape(tok_count, head_count, HD)
    first_seg = seg_tok[0]
    last_seg = seg_tok[-1]
    own_segs = jnp.stack([first_seg + 1, last_seg + 1]).astype(jnp.float32)
    in_last = (seg_tok == last_seg)[:, None, None]
    own_kv = jnp.einsum(
        "thd,the->hde",
        jnp.where(in_last, flat_k, jnp.zeros_like(flat_k)),
        flat_v,
        preferred_element_type=jnp.float32,
    )
    empty = (jnp.zeros_like(own_kv), jnp.zeros((2,), jnp.float32))

    def relay_step(step_index, incoming):
        return shifted(join_forward(incoming, (own_kv, own_segs)), "context", 1)

    arrived = lax.fori_loop(0, lax.axis_size("context") - 1, relay_step, empty)
    state_in = jnp.where(arrived[1][1] == own_segs[0], arrived[0], 0.0)
    block_q = flat_q.reshape(block_count, BLK, head_count, HD)
    block_k = flat_k.reshape(block_count, BLK, head_count, HD)
    block_v = flat_v.reshape(block_count, BLK, head_count, HD)
    final, stored = lax.scan(
        forward_block, (state_in, first_seg), (block_q, block_k, block_v, seg_blocks)
    )
    attended_blocks, weights_all, state_all, prev_all = stored
    attended = attended_blocks.reshape(tok_count, local_width)
    cotangent = grad_out[0].astype(jnp.float32)
    gained = cotangent * norm_gain
    squares, inner = lax.psum(
        (jnp.sum(attended * attended, axis=1), jnp.sum(gained * attended, axis=1)), "tensor"
    )
    radius = jnp.sqrt(squares / WIDTH + 1e-06)
    normed = attended / radius[:, None]
    normed_out = (normed * norm_gain).astype(jnp.bfloat16)
    grad_gain = lax.psum(jnp.sum(cotangent * normed, axis=0), ("context", "dp"))
    grad_att = (
        (gained - attended * (inner / (WIDTH * radius * radius))[:, None]) / radius[:, None]
    ).astype(jnp.bfloat16)
    flat_da = grad_att.reshape(tok_count, head_count, HD)
    in_first = (seg_tok == first_seg)[:, None, None]
    own_grad = jnp.einsum(
        "thd,the->hde",
        jnp.where(in_first, flat_q, jnp.zeros_like(flat_q)),
        flat_da,
        preferred_element_type=jnp.float32,
    )
    behind = prefix((own_grad, own_segs), "context", join_backward, empty)
    grad_in = jnp.where(behind[1][0] == own_segs[1], behind[0], 0.0)
    block_da = flat_da.reshape(block_count, BLK, head_count, HD)
    leftover, grads = lax.scan(
        backward_block,
        grad_in,
        (block_q, block_k, block_v, seg_blocks, block_da, weights_all, state_all, prev_all),
        reverse=True,
    )
    grad_queries = grads[0].reshape(1, tok_count, local_width)
    grad_keys = grads[1].reshape(1, tok_count, local_width)
    grad_values = grads[2].reshape(1, tok_count, local_width)
    return (
        normed_out.reshape(1, tok_count, local_width),
        grad_queries,
        grad_keys,
        grad_values,
        grad_gain,
    )


def solution(mesh):
    in_specs = (
        P("dp", "context", "tensor"),
        P("dp", "context", "tensor"),
        P("dp", "context", "tensor"),
        P("tensor"),
        P("dp", "context"),
        P("dp", "context", "tensor"),
    )
    out_specs = (
        P("dp", "context", "tensor"),
        P("dp", "context", "tensor"),
        P("dp", "context", "tensor"),
        P("dp", "context", "tensor"),
        P("tensor"),
    )
    return jax.shard_map(body, mesh=mesh, in_specs=in_specs, out_specs=out_specs, check_vma=False)
```

profile of v0, /device:TPU:0, one launch (start us, length us, event | category | flops | bytes accessed | tf_op | source)
XLA Modules:
  0.0 330.4 jit_solution(14289737301600793897)
XLA Ops:
  20.1 50.7 %while.71 = (s32[]{:T(128)}, f32[8,128,128]{2,1,0:T(8,128)S(1)}, f32[2]{0:T(128)S(1)}, f32[2]{0:T(128)S(1)}, pred[]{:T(512)}, /*index=5*/pred[]{:T(512)}, f32[8,...) while((s32[]{:T(128)}, f32[8,128,128]{2,1,0:T(8,128)S(1)}, f32[2]{0:T(128)S(1)}, f32[2]{0:T(128)S(1)}, ...), condition=%wide.region_1.2_spmd, body=%wide.region_0.1_spmd.sunk | while | flops 262154 | bytes 3670328 | solution.py:153
  22.2 5.0 %collective-permute-start = (f32[8,128,128]{2,1,0:T(8,128)S(1)}, f32[8,128,128]{2,1,0:T(8,128)S(1)}, u32[]{:S(2)}, u32[]{:S(2)}) collective-permute-start(f32[8,128,128]{2,1,0:T(8,128)S(1)} %select_add_fusion.2), channel_id=1, source_target_pairs={{0,8},{8,16},{16,24},{1,9},{9,17},{17,25},{2,10},{10,18},{18,26},{... | collective-permute-start | bytes 1572872 | tf_op jit(solution)/shard_map/while/body/eval_jaxpr/ppermute | solution.py:15
  30.5 3.4 %collective-permute-start.1 = (f32[2]{0:T(128)S(1)}, f32[2]{0:T(128)S(1)}, u32[]{:S(2)}, u32[]{:S(2)}) collective-permute-start(f32[2]{0:T(128)S(1)} %pad_maximum_fusion.2), channel_id=1, source_target_pairs={{0,8},{8,16},{16,24},{1,9},{9,17},{17,25},{2,10},{10,18},{18,26},{... | collective-permute-start | bytes 32 | tf_op jit(solution)/shard_map/while/body/eval_jaxpr/ppermute | solution.py:15
  33.9 4.4 %collective-permute-done.1 = f32[2]{0:T(128)S(1)} collective-permute-done((f32[2]{0:T(128)S(1)}, f32[2]{0:T(128)S(1)}, u32[]{:S(2)}, u32[]{:S(2)}) %collective-permute-start.1) | collective-permute-done | bytes 40 | tf_op jit(solution)/shard_map/while/body/eval_jaxpr/ppermute | solution.py:15
  40.4 4.4 %collective-permute-start = (f32[8,128,128]{2,1,0:T(8,128)S(1)}, f32[8,128,128]{2,1,0:T(8,128)S(1)}, u32[]{:S(2)}, u32[]{:S(2)}) collective-permute-start(f32[8,128,128]{2,1,0:T(8,128)S(1)} %select_add_fusion.2), channel_id=1, source_target_pairs={{0,8},{8,16},{16,24},{1,9},{9,17},{17,25},{2,10},{10,18},{18,26},{... | collective-permute-start | bytes 1572872 | tf_op jit(solution)/shard_map/while/body/eval_jaxpr/ppermute | solution.py:15
  48.2 3.4 %collective-permute-start.1 = (f32[2]{0:T(128)S(1)}, f32[2]{0:T(128)S(1)}, u32[]{:S(2)}, u32[]{:S(2)}) collective-permute-start(f32[2]{0:T(128)S(1)} %pad_maximum_fusion.2), channel_id=1, source_target_pairs={{0,8},{8,16},{16,24},{1,9},{9,17},{17,25},{2,10},{10,18},{18,26},{... | collective-permute-start | bytes 32 | tf_op jit(solution)/shard_map/while/body/eval_jaxpr/ppermute | solution.py:15
  51.6 3.5 %collective-permute-done.1 = f32[2]{0:T(128)S(1)} collective-permute-done((f32[2]{0:T(128)S(1)}, f32[2]{0:T(128)S(1)}, u32[]{:S(2)}, u32[]{:S(2)}) %collective-permute-start.1) | collective-permute-done | bytes 40 | tf_op jit(solution)/shard_map/while/body/eval_jaxpr/ppermute | solution.py:15
  57.2 4.4 %collective-permute-start = (f32[8,128,128]{2,1,0:T(8,128)S(1)}, f32[8,128,128]{2,1,0:T(8,128)S(1)}, u32[]{:S(2)}, u32[]{:S(2)}) collective-permute-start(f32[8,128,128]{2,1,0:T(8,128)S(1)} %select_add_fusion.2), channel_id=1, source_target_pairs={{0,8},{8,16},{16,24},{1,9},{9,17},{17,25},{2,10},{10,18},{18,26},{... | collective-permute-start | bytes 1572872 | tf_op jit(solution)/shard_map/while/body/eval_jaxpr/ppermute | solution.py:15
  64.9 3.4 %collective-permute-start.1 = (f32[2]{0:T(128)S(1)}, f32[2]{0:T(128)S(1)}, u32[]{:S(2)}, u32[]{:S(2)}) collective-permute-start(f32[2]{0:T(128)S(1)} %pad_maximum_fusion.2), channel_id=1, source_target_pairs={{0,8},{8,16},{16,24},{1,9},{9,17},{17,25},{2,10},{10,18},{18,26},{... | collective-permute-start | bytes 32 | tf_op jit(solution)/shard_map/while/body/eval_jaxpr/ppermute | solution.py:15
  68.4 2.5 collective-permute-done.1
  74.2 3.1 copy.106
  80.4 31.8 %while.72 = (s32[]{:T(128)}, f32[8,128,128]{2,1,0:T(8,128)S(1)}, s32[]{:T(128)}, f32[3,256,8,128]{1,3,2,0:T(8,128)}, bf16[3,8,256,256]{3,2,1,0:T(8,128)(2,1)}, /...) while((s32[]{:T(128)}, f32[8,128,128]{2,1,0:T(8,128)S(1)}, ...), condition=%wide.region_3.4_spmd, body=%wide.region_2.3_spmd.sunk | while | flops 405209600 | bytes 18224672 | solution.py:158
  86.3 2.4 fusion.112
  96.9 2.4 fusion.112
  107.5 2.4 fusion.112
  113.4 2.5 copy.70
  118.1 2.6 copy.93
  126.4 2.5 all-reduce
  128.9 4.9 %fusion.54 = bf16[768,8,128]{2,1,0:T(8,128)(2,1)S(1)} fusion(f32[96,8,8,128]{3,2,1,0:T(8,128)} %copy-done.6, f32[3,256,8,128]{3,2,1,0:T(8,128)S(1)} %copy.70, f32[768]{0:T(1024)S(1)} %get-tuple-element.728, f32[768]{0:T(1024)S(1)} %get-tuple-element.727, f32[8,128]{1,0:T(8,128)S(1)} %bitcast.320), kind=kLoop, calls=%fused_computation.98 | loop fusion | flops 3932160 | bytes 7874560 | tf_op jit(solution)/shard_map/convert_element_type | solution.py:174
  135.3 12.0 %all-gather.1 = f32[4,1,2]{2,1,0:T(1,128)S(1)} all-gather(f32[1,1,2]{2,1,0:T(1,128)S(1)} %fusion.66), channel_id=1, replica_groups=mesh['context'=4,'tensor'=2,'dp'=4] {'context'}, dimensions={0}, use_global_device_ids=true | all-gather | bytes 40 | tf_op jit(solution)/shard_map/all_gather | solution.py:20
  147.4 2.4 reshape.302
  149.8 2.4 fusion.51
  152.2 39.9 %psum.23 = f32[1024]{0:T(1024)} all-reduce(f32[1024]{0:T(1024)S(1)} %fusion.51), channel_id=1, replica_groups=mesh['context'=4,'tensor'=2,'dp'=4] {'context','dp'}, use_global_device_ids=true, to_apply=%region_13.14 | all-reduce | flops 1024 | bytes 8192 | tf_op jit(solution)/shard_map/psum | solution.py:171
  192.2 3.7 %multiply_convert_fusion = bf16[1,768,1024]{2,1,0:T(8,128)(2,1)} fusion(f32[1,768,1024]{2,1,0:T(8,128)} %reshape.302, f32[1024]{0:T(1024)S(1)} %copy-done.15, f32[768]{0:T(1024)S(1)} %get-tuple-element.728), kind=kLoop, calls=%fused_computation.102 | loop fusion | flops 2359296 | bytes 4725760 | tf_op jit(solution)/shard_map/convert_element_type | solution.py:170
  195.9 2.9 divide_convert_fusion
  198.8 39.5 %while.74 = (s32[]{:T(128)}, f32[8,128,128]{2,1,0:T(8,128)}, f32[2]{0:T(128)S(1)}, s32[]{:T(128)}, f32[4,8,128,128]{3,2,1,0:T(8,128)}, /*index=5*/f32[4,2]{0,1:T...) while((s32[]{:T(128)}, f32[8,128,128]{2,1,0:T(8,128)}, ...), condition=%wide.region_9.10_spmd.clone, body=%wide.region_8.9_spmd.clone.sunk | while | flops 524312 | bytes 1573215 | solution.py:33
  244.1 71.5 %while.73 = (s32[]{:T(128)}, f32[8,128,128]{2,1,0:T(8,128)S(1)}, bf16[3,256,8,128]{3,2,1,0:T(8,128)(2,1)}, bf16[3,256,8,128]{3,2,1,0:T(8,128)(2,1)}, bf16[3,256,...) while((s32[]{:T(128)}, f32[8,128,128]{2,1,0:T(8,128)S(1)}, ...), condition=%wide.region_11.12_spmd, body=%wide.region_10.11_spmd.sunk | while | flops 809697792 | bytes 39720800 | solution.py:186
  245.3 2.5 select_convert_fusion.3
  253.4 2.2 fusion.128
  269.2 2.5 select_convert_fusion.3
  293.0 2.5 select_convert_fusion.3
  315.7 3.8 %reshape.304 = bf16[1,768,1024]{2,1,0:T(8,128)(2,1)} reshape(bf16[3,256,8,128]{3,2,1,0:T(8,128)(2,1)} %get-tuple-element.544) | data formatting | bytes 3145728 | tf_op jit(solution)/shard_map/reshape | solution.py:192
  (232 shorter events, 128.2 us)
Async XLA Ops:
  7.2 191.7 %all-gather.4.cloned.1.call-start = ((), (), s32[]{:S(2)}) async-start(), calls=%async_computation | async-start | bytes 2621440 | tf_op jit(solution)/shard_map/all_gather | solution.py:20
  14.4 2.0 copy-start.8
  16.4 1.7 copy-start.10
  20.1 53.1 %copy-start.16 = (s32[1,12]{1,0:T(1,128)S(1)}, s32[1,12]{1,0:T(1,128)}, u32[]{:S(2)}) copy-start(s32[1,12]{1,0:T(1,128)} %param.18) | copy-start | bytes 148
  22.2 16.1 %collective-permute-start = (f32[8,128,128]{2,1,0:T(8,128)S(1)}, f32[8,128,128]{2,1,0:T(8,128)S(1)}, u32[]{:S(2)}, u32[]{:S(2)}) collective-permute-start(f32[8,128,128]{2,1,0:T(8,128)S(1)} %select_add_fusion.2), channel_id=1, source_target_pairs={{0,8},{8,16},{16,24},{1,9},{9,17},{17,25},{2,10},{10,18},{18,26},{... | collective-permute-start | bytes 1572872 | tf_op jit(solution)/shard_map/while/body/eval_jaxpr/ppermute | solution.py:15
  30.5 7.9 %collective-permute-start.1 = (f32[2]{0:T(128)S(1)}, f32[2]{0:T(128)S(1)}, u32[]{:S(2)}, u32[]{:S(2)}) collective-permute-start(f32[2]{0:T(128)S(1)} %pad_maximum_fusion.2), channel_id=1, source_target_pairs={{0,8},{8,16},{16,24},{1,9},{9,17},{17,25},{2,10},{10,18},{18,26},{... | collective-permute-start | bytes 32 | tf_op jit(solution)/shard_map/while/body/eval_jaxpr/ppermute | solution.py:15
  40.4 14.7 %collective-permute-start = (f32[8,128,128]{2,1,0:T(8,128)S(1)}, f32[8,128,128]{2,1,0:T(8,128)S(1)}, u32[]{:S(2)}, u32[]{:S(2)}) collective-permute-start(f32[8,128,128]{2,1,0:T(8,128)S(1)} %select_add_fusion.2), channel_id=1, source_target_pairs={{0,8},{8,16},{16,24},{1,9},{9,17},{17,25},{2,10},{10,18},{18,26},{... | collective-permute-start | bytes 1572872 | tf_op jit(solution)/shard_map/while/body/eval_jaxpr/ppermute | solution.py:15
  48.2 6.9 %collective-permute-start.1 = (f32[2]{0:T(128)S(1)}, f32[2]{0:T(128)S(1)}, u32[]{:S(2)}, u32[]{:S(2)}) collective-permute-start(f32[2]{0:T(128)S(1)} %pad_maximum_fusion.2), channel_id=1, source_target_pairs={{0,8},{8,16},{16,24},{1,9},{9,17},{17,25},{2,10},{10,18},{18,26},{... | collective-permute-start | bytes 32 | tf_op jit(solution)/shard_map/while/body/eval_jaxpr/ppermute | solution.py:15
  57.2 13.7 %collective-permute-start = (f32[8,128,128]{2,1,0:T(8,128)S(1)}, f32[8,128,128]{2,1,0:T(8,128)S(1)}, u32[]{:S(2)}, u32[]{:S(2)}) collective-permute-start(f32[8,128,128]{2,1,0:T(8,128)S(1)} %select_add_fusion.2), channel_id=1, source_target_pairs={{0,8},{8,16},{16,24},{1,9},{9,17},{17,25},{2,10},{10,18},{18,26},{... | collective-permute-start | bytes 1572872 | tf_op jit(solution)/shard_map/while/body/eval_jaxpr/ppermute | solution.py:15
  64.9 5.9 %collective-permute-start.1 = (f32[2]{0:T(128)S(1)}, f32[2]{0:T(128)S(1)}, u32[]{:S(2)}, u32[]{:S(2)}) collective-permute-start(f32[2]{0:T(128)S(1)} %pad_maximum_fusion.2), channel_id=1, source_target_pairs={{0,8},{8,16},{16,24},{1,9},{9,17},{17,25},{2,10},{10,18},{18,26},{... | collective-permute-start | bytes 32 | tf_op jit(solution)/shard_map/while/body/eval_jaxpr/ppermute | solution.py:15
  74.2 3.1 copy-start.11
  77.3 1.4 copy-start.9
  82.4 1.6 copy-start.3
  82.4 1.6 copy-start.4
  93.0 1.6 copy-start.3
  93.0 1.6 copy-start.4
  103.6 1.6 copy-start.3
  103.6 1.6 copy-start.4
  112.2 1.3 copy-start.1
  122.5 2.4 copy-start.15
  123.3 1.7 copy-start.6
  128.9 4.9 %copy-start.14 = (bf16[1,768,1024]{1,2,0:T(8,128)(2,1)S(1)}, bf16[1,768,1024]{1,2,0:T(8,128)(2,1)}, u32[]{:S(2)}) copy-start(bf16[1,768,1024]{1,2,0:T(8,128)(2,1)} %copy.93) | copy-start | bytes 4718596
  192.2 3.7 %copy-start.7 = (f32[96,8,8,128]{3,2,1,0:T(8,128)S(1)}, f32[96,8,8,128]{3,2,1,0:T(8,128)}, u32[]{:S(2)}) copy-start(f32[96,8,8,128]{3,2,1,0:T(8,128)} %copy-done.6) | copy-start | bytes 9437188
  261.5 1.8 copy-start
  265.1 1.5 copy-start.2
  285.3 1.8 copy-start
  288.9 1.5 copy-start.2
  309.1 1.8 copy-start
  312.7 1.2 copy-start.5
  312.7 1.5 copy-start.2
  315.7 3.8 %copy-start.12 = (bf16[3,256,8,128]{3,2,1,0:T(8,128)(2,1)S(1)}, bf16[3,256,8,128]{3,2,1,0:T(8,128)(2,1)}, u32[]{:S(2)}) copy-start(bf16[3,256,8,128]{3,2,1,0:T(8,128)(2,1)} %get-tuple-element.545) | copy-start | bytes 4718596
  319.5 2.0 copy-start.13
  (2 other events, 2.4 us)
Sparse Core Ops, SparseCore 0:
  135.4 48.6 all-gather.3
where the time goes:
time: 334 us; the launch traced here: 330 us
  local copies, waits for them, and re-layouts  78.9 us (24%)
  blocking collectives  54.4 us (16%)
  matrix products  54.3 us (16%)
  loops' own time  48.1 us (14%)
  other arithmetic  40.1 us (12%)
  starting transfers between devices  24.2 us (7%)
  between operations  20 us (6%)
  waiting for transfers between devices  10.4 us (3%)
    psum x1, blocking collectives, body(): grad_gain = lax.psum(jnp.sum(cotangent * normed, axis=0), ('context', 'dp'))  39.9 us
    another operation x1, loops' own time, prefix(): return lax.fori_loop(0, size, step, start)  25.8 us
    ppermute x6, starting transfers between devices, shifted(): return lax.ppermute(block, axis, route)  24.2 us
    dynamic_slice x24, local copies, waits for them, and re-layouts, body(): lax.scan(forward_block, (state_in, first_seg), (block_q, block_k, block_v...  20.9 us
    another operation x1, loops' own time, body(): arrived = lax.fori_loop(0, lax.axis_size('context') - 1, relay_step, empty)  13.8 us
    all_gather x1, blocking collectives, prefix(): everything = jax.tree.map(lambda part: lax.all_gather(part, axis), value)  12 us
    unnamed x29, local copies, waits for them, and re-layouts  11.9 us
    ppermute x6, waiting for transfers between devices, shifted(): return lax.ppermute(block, axis, route)  10.4 us
  transfers between devices with their start and end apart: 7, of which 3 were waited for; matrix products, arithmetic and copies ran while one was open for 4% of the time, Pallas kernels for 0%

commit v1 on v0

v1 whole, which is shorter than its diff:
```python
import functools

import jax
import jax.numpy as jnp
from jax import lax
from jax.experimental import pallas as pl
from jax.experimental.pallas import tpu as pltpu
from jax.sharding import PartitionSpec as P

HD = 128
BLK = 256
SEGB = 64
PER = BLK // SEGB
F32 = jnp.float32
BF16 = jnp.bfloat16
MESH = pl.DeviceIdType.MESH


def nn(a, b):
    return lax.dot_general(a, b, (((1,), (0,)), ((), ())), preferred_element_type=F32)


def nt(a, b):
    return lax.dot_general(a, b, (((1,), (1,)), ((), ())), preferred_element_type=F32)


def tn(a, b):
    return lax.dot_general(a, b, (((0,), (0,)), ((), ())), preferred_element_type=F32)


def flag(cond):
    return jnp.where(cond, 1.0, 0.0).astype(F32)


def spread(index, ids):
    out = jnp.full(index.shape, ids[-1], jnp.int32)
    for i in reversed(range(len(ids) - 1)):
        out = jnp.where(index < (i + 1) * SEGB, ids[i], out)
    return out


def kernel(
    nctx, ndp, heads, blocks, width,
    seg_ref, gain_ref, q_hbm, k_hbm, v_hbm, g_hbm,
    no_hbm, gq_hbm, gk_hbm, gv_hbm, gg_ref,
    qs, ks, vs, gs, no_s, gq_s, gk_s, gv_s,
    att, weights, datt, visible, mprev, mlast,
    local, state_bf, s_in, s_out, grad_local, g_in, g_out,
    sq_acc, in_acc, tile_out, tile_in, sums_out, sums_in,
    gg_part, gg_dp, gg_ctx_out, gg_ctx,
    in_sem, out_sem, fs_sem, fr_sem, bs_sem, br_sem, ts_sem, tr_sem,
    xs_sem, xr_sem, ds_sem, dr_sem, cs_sem, cr_sem,
):
    ctx = lax.axis_index("context")
    ten = lax.axis_index("tensor")
    dp = lax.axis_index("dp")
    toks = blocks * BLK
    last = nctx - 1

    def in_copy(n, src, dst, h):
        cols = pl.ds(pl.multiple_of(h * HD, HD), HD)
        return pltpu.make_async_copy(src.at[0, :, cols], dst.at[h], in_sem.at[n, h])

    def out_copy(n, src, dst, h):
        cols = pl.ds(pl.multiple_of(h * HD, HD), HD)
        return pltpu.make_async_copy(src.at[h], dst.at[0, :, cols], out_sem.at[n, h])

    ins = ((k_hbm, ks), (v_hbm, vs), (q_hbm, qs), (g_hbm, gs))
    outs = ((no_s, no_hbm), (gq_s, gq_hbm), (gk_s, gk_hbm), (gv_s, gv_hbm))

    @pl.loop(0, heads)
    def _(h):
        for n in (0, 1):
            in_copy(n, *ins[n], h).start()

    @pl.loop(0, heads)
    def _(h):
        for n in (2, 3):
            in_copy(n, *ins[n], h).start()

    barrier = pltpu.get_barrier_semaphore()
    pl.semaphore_signal(barrier, inc=1, device_id={"tensor": 1 - ten}, device_id_type=MESH)

    @pl.loop(1, ndp)
    def _(d):
        pl.semaphore_signal(
            barrier, inc=1, device_id={"dp": lax.rem(dp + d, ndp)}, device_id_type=MESH
        )

    @pl.loop(1, nctx)
    def _(d):
        pl.semaphore_signal(
            barrier, inc=1, device_id={"context": lax.rem(ctx + d, nctx)}, device_id_type=MESH
        )

    seg = [[seg_ref[0, j * PER + i] for i in range(PER)] for j in range(blocks)]
    lasts = [seg[j][-1] for j in range(blocks)]
    tile_out[...] = jnp.full((8, HD), lasts[-1], jnp.int32).astype(F32)
    rows = lax.broadcasted_iota(jnp.int32, (BLK, BLK), 0)
    cols = lax.broadcasted_iota(jnp.int32, (BLK, BLK), 1)
    rows_h = lax.broadcasted_iota(jnp.int32, (BLK, HD), 0)
    for j in range(blocks):
        same = spread(rows, seg[j]) == spread(cols, seg[j])
        visible[j] = flag(jnp.logical_and(rows >= cols, same))
        seg_h = spread(rows_h, seg[j])
        at = pl.ds(j * BLK, BLK)
        mlast[at, :] = flag(seg_h == lasts[j]).astype(BF16)
        before = seg[0][0] if j == 0 else lasts[j - 1]
        mprev[at, :] = flag(seg_h == before).astype(BF16)
    step = [flag(seg[0][0] == lasts[0])]
    for j in range(1, blocks):
        step.append(flag(lasts[j - 1] == lasts[j]))

    pl.semaphore_wait(barrier, 1 + (ndp - 1) + (nctx - 1))

    def tile_copy():
        return pltpu.make_async_remote_copy(
            tile_out, tile_in, ts_sem, tr_sem,
            device_id={"context": jnp.minimum(ctx + 1, last)}, device_id_type=MESH,
        )

    def fwd_copy(h):
        return pltpu.make_async_remote_copy(
            s_out.at[h], s_in.at[h], fs_sem.at[h], fr_sem.at[h],
            device_id={"context": jnp.minimum(ctx + 1, last)}, device_id_type=MESH,
        )

    def bwd_copy(h):
        return pltpu.make_async_remote_copy(
            g_out.at[h], g_in.at[h], bs_sem.at[h], br_sem.at[h],
            device_id={"context": jnp.maximum(ctx - 1, 0)}, device_id_type=MESH,
        )

    @pl.when(ctx < last)
    def _():
        tile_copy().start()

    @pl.when(ctx == 0)
    def _():
        s_in[...] = jnp.zeros_like(s_in)
        tile_in[...] = jnp.full((8, HD), -1.0, F32)

    @pl.when(ctx == last)
    def _():
        g_in[...] = jnp.zeros_like(g_in)

    def rows_of(j):
        return pl.ds(j * BLK, BLK)

    @pl.loop(0, heads)
    def _(h):
        for n in (0, 1):
            in_copy(n, *ins[n], h).wait()
        run = None
        for j in range(blocks):
            km = ks[h, rows_of(j), :] * mlast[rows_of(j), :]
            add = tn(km, vs[h, rows_of(j), :])
            run = add if run is None else run * step[j] + add
            local[h, j] = run

        @pl.when(jnp.logical_and(ctx == 0, ctx < last))
        def _():
            s_out[h] = local[h, blocks - 1]
            fwd_copy(h).start()

    @pl.when(ctx > 0)
    def _():
        tile_copy().wait_recv()

    match = flag(tile_in[0:1, :] == jnp.full((1, HD), seg[0][0], jnp.int32).astype(F32))
    mprev[rows_of(0), :] = (mprev[rows_of(0), :].astype(F32) * match).astype(BF16)
    reach = [match * step[0]]
    for j in range(1, blocks):
        reach.append(reach[-1] * step[j])

    sq_acc[...] = jnp.zeros_like(sq_acc)
    in_acc[...] = jnp.zeros_like(in_acc)

    @pl.loop(0, heads)
    def _(h):
        @pl.when(ctx > 0)
        def _():
            fwd_copy(h).wait_recv()

        @pl.when(jnp.logical_and(ctx > 0, ctx < last))
        def _():
            s_out[h] = local[h, blocks - 1] + s_in[h] * reach[-1]
            fwd_copy(h).start()

        for n in (2, 3):
            in_copy(n, *ins[n], h).wait()
        gain = gain_ref[pl.ds(h, 1), :]
        for j in range(blocks):
            at = rows_of(j)
            q = qs[h, at, :]
            came = s_in[h]
            state = came if j == 0 else local[h, j - 1] + came * reach[j - 1]
            state = state.astype(BF16)
            state_bf[h, j] = state
            w = (nt(q, ks[h, at, :]) * visible[j]).astype(BF16)
            weights[h, j] = w
            a = nn(w, vs[h, at, :]) + nn(q * mprev[at, :], state)
            att[h, at, :] = a
            sq_acc[at, :] += a * a
            in_acc[at, :] += a * (gs[h, at, :].astype(F32) * gain)

    groups = toks // HD
    eye = (
        lax.broadcasted_iota(jnp.int32, (HD, HD), 0) == lax.broadcasted_iota(jnp.int32, (HD, HD), 1)
    )
    for n, acc in ((0, sq_acc), (1, in_acc)):
        for i in range(groups):
            col = jnp.sum(acc[pl.ds(i * HD, HD), :], axis=1, keepdims=True)
            row = jnp.sum(
                jnp.where(eye, jnp.broadcast_to(col, (HD, HD)), 0.0), axis=0, keepdims=True
            )
            sums_out[n, pl.ds(i, 1), :] = row
    swap = pltpu.make_async_remote_copy(
        sums_out, sums_in, xs_sem, xr_sem, device_id={"tensor": 1 - ten}, device_id_type=MESH
    )
    swap.start()
    swap.wait()
    for i in range(groups):
        at = pl.ds(i * HD, HD)
        cols2 = []
        for n in (0, 1):
            row = sums_out[n, pl.ds(i, 1), :] + sums_in[n, pl.ds(i, 1), :]
            cols2.append(
                jnp.sum(
                    jnp.where(eye, jnp.broadcast_to(row, (HD, HD)), 0.0), axis=1, keepdims=True
                )
            )
        mean = cols2[0] / width + 1e-06
        radius = jnp.sqrt(mean)
        sq_acc[at, :] = jnp.broadcast_to(1.0 / radius, (HD, HD))
        in_acc[at, :] = jnp.broadcast_to(cols2[1] / (width * radius * radius), (HD, HD))

    @pl.loop(0, heads)
    def _(h):
        gain = gain_ref[pl.ds(h, 1), :]
        total = jnp.zeros((1, HD), F32)
        adds = []
        for j in range(blocks):
            at = rows_of(j)
            inv = sq_acc[at, :]
            a = att[h, at, :]
            g = gs[h, at, :].astype(F32)
            normed = a * inv
            no_s[h, at, :] = (normed * gain).astype(BF16)
            total = total + jnp.sum(g * normed, axis=0, keepdims=True)
            d = ((g * gain - a * in_acc[at, :]) * inv).astype(BF16)
            datt[h, at, :] = d
            adds.append(tn(qs[h, at, :] * mprev[at, :], d))
        gg_part[pl.ds(h, 1), :] = total
        run = None
        for j in reversed(range(blocks)):
            run = adds[j] if run is None else adds[j] + run * (match * step[0] if j == 0 else step[j])
            grad_local[h, j] = run
        out_copy(0, *outs[0], h).start()

        @pl.when(jnp.logical_and(ctx == last, ctx > 0))
        def _():
            g_out[h] = grad_local[h, 0]
            bwd_copy(h).start()

    gg_dp[dp] = gg_part[...]

    def dp_copy(to, slot):
        return pltpu.make_async_remote_copy(
            gg_part, gg_dp.at[slot], ds_sem.at[to], dr_sem.at[slot],
            device_id={"dp": to}, device_id_type=MESH,
        )

    def ctx_copy(to, slot):
        return pltpu.make_async_remote_copy(
            gg_ctx_out, gg_ctx.at[slot], cs_sem.at[to], cr_sem.at[slot],
            device_id={"context": to}, device_id_type=MESH,
        )

    @pl.loop(1, ndp)
    def _(d):
        dp_copy(lax.rem(dp + d, ndp), dp).start()

    full = [None] * (blocks + 1)
    full[blocks] = 1.0
    for j in reversed(range(blocks)):
        full[j] = full[j + 1] * (match * step[0] if j == 0 else step[j])

    @pl.loop(0, heads)
    def _(h):
        @pl.when(ctx < last)
        def _():
            bwd_copy(h).wait_recv()

        @pl.when(jnp.logical_and(ctx < last, ctx > 0))
        def _():
            g_out[h] = grad_local[h, 0] + g_in[h] * full[0]
            bwd_copy(h).start()

        came = g_in[h]
        for j in range(blocks):
            at = rows_of(j)
            grad = came if j == blocks - 1 else grad_local[h, j + 1] + came * full[j + 1]
            grad = grad.astype(BF16)
            d = datt[h, at, :]
            k = ks[h, at, :]
            v = vs[h, at, :]
            mp = mprev[at, :]
            ml = mlast[at, :]
            dw = (nt(d, v) * visible[j]).astype(BF16)
            gq = nn(dw, k) + nt(d * mp, state_bf[h, j])
            gq_s[h, at, :] = gq.astype(BF16)
            gk = tn(dw, qs[h, at, :]) + nt(v * ml, grad)
            gk_s[h, at, :] = gk.astype(BF16)
            gv = tn(weights[h, j], d) + nn(k * ml, grad)
            gv_s[h, at, :] = gv.astype(BF16)
        for n in (1, 2, 3):
            out_copy(n, *outs[n], h).start()

        @pl.when(h == heads // 2)
        def _():
            @pl.loop(1, ndp)
            def _(d):
                peer = lax.rem(dp + d, ndp)
                dp_copy(peer, peer).wait_recv()

            part = gg_dp[0]
            for i in range(1, ndp):
                part = part + gg_dp[i]
            gg_ctx_out[...] = part
            gg_ctx[ctx] = part

            @pl.loop(1, nctx)
            def _(d):
                ctx_copy(lax.rem(ctx + d, nctx), ctx).start()

    @pl.loop(1, nctx)
    def _(d):
        peer = lax.rem(ctx + d, nctx)
        ctx_copy(peer, peer).wait()

    gg_ref[...] = lax.fori_loop(
        1, nctx, lambda i, total: total + gg_ctx[i], gg_ctx[0]
    )

    @pl.loop(1, ndp)
    def _(d):
        peer = lax.rem(dp + d, ndp)
        dp_copy(peer, peer).wait_send()

    @pl.when(ctx < last)
    def _():
        tile_copy().wait_send()

        @pl.loop(0, heads)
        def _(h):
            fwd_copy(h).wait_send()

    @pl.when(ctx > 0)
    def _():
        @pl.loop(0, heads)
        def _(h):
            bwd_copy(h).wait_send()

    @pl.loop(0, heads)
    def _(h):
        for n in range(4):
            out_copy(n, *outs[n], h).wait()


def body(nctx, ndp, full_width, queries, keys_in, values, norm_gain, segment_ids, grad_out):
    toks, local_width = queries.shape[1:]
    heads = local_width // HD
    blocks = toks // BLK
    wide = jax.ShapeDtypeStruct(queries.shape, BF16)
    hbm = pl.BlockSpec(memory_space=pl.ANY)
    vmem = pl.BlockSpec(memory_space=pltpu.VMEM)
    per_head = pltpu.VMEM((heads, toks, HD), BF16)
    states = pltpu.VMEM((heads, blocks, HD, HD), F32)
    hops = pltpu.VMEM((heads, HD, HD), F32)
    rowish = pltpu.VMEM((toks, HD), F32)
    dma = pltpu.SemaphoreType.DMA
    groups = -(-(toks // HD) // 8) * 8
    sums = pltpu.VMEM((2, groups, HD), F32)
    part = pltpu.VMEM((heads, HD), F32)
    outs = pl.pallas_call(
        functools.partial(kernel, nctx, ndp, heads, blocks, full_width),
        out_shape=[wide] * 4 + [jax.ShapeDtypeStruct((heads, HD), F32)],
        in_specs=[pl.BlockSpec(memory_space=pltpu.SMEM), vmem] + [hbm] * 4,
        out_specs=[hbm] * 4 + [vmem],
        scratch_shapes=[per_head] * 8
        + [
            pltpu.VMEM((heads, toks, HD), F32),
            pltpu.VMEM((heads, blocks, BLK, BLK), BF16),
            per_head,
            pltpu.VMEM((blocks, BLK, BLK), F32),
            pltpu.VMEM((toks, HD), BF16),
            pltpu.VMEM((toks, HD), BF16),
            states,
            pltpu.VMEM((heads, blocks, HD, HD), BF16),
            hops, hops, states, hops, hops,
            rowish, rowish,
            pltpu.VMEM((8, HD), F32), pltpu.VMEM((8, HD), F32),
            sums, sums,
            part,
            pltpu.VMEM((ndp, heads, HD), F32),
            part,
            pltpu.VMEM((nctx, heads, HD), F32),
            dma((4, heads)), dma((4, heads)),
            dma((heads,)), dma((heads,)), dma((heads,)), dma((heads,)),
            dma, dma, dma, dma,
            dma((ndp,)), dma((ndp,)), dma((nctx,)), dma((nctx,)),
        ],
        compiler_params=pltpu.CompilerParams(
            collective_id=0, has_side_effects=True, vmem_limit_bytes=56 << 20
        ),
    )(segment_ids, norm_gain.reshape(heads, HD), queries, keys_in, values, grad_out)
    return (*outs[:4], outs[4].reshape(local_width))


def solution(mesh):
    wide = P("dp", "context", "tensor")
    in_specs = (wide, wide, wide, P("tensor"), P("dp", "context"), wide)
    out_specs = (wide, wide, wide, wide, P("tensor"))

    def run(queries, *rest):
        fn = functools.partial(
            body, mesh.shape["context"], mesh.shape["dp"], queries.shape[2]
        )
        return jax.shard_map(
            fn, mesh=mesh, in_specs=in_specs, out_specs=out_specs, check_vma=False
        )(queries, *rest)

    return run
```

time: 334 us -> 62.5 us (0.19); the launches traced: 330 us -> 62.3 us
  local copies, waits for them, and re-layouts: 78.9 us -> 8.48 us
  blocking collectives: 54.4 us -> 0 us
  matrix products: 54.3 us -> 0 us
  Pallas kernels: 0 us -> 53.1 us
  loops' own time: 48.1 us -> 0 us
  other arithmetic: 40.1 us -> 0 us
  starting transfers between devices: 24.2 us -> 0 us
  between operations: 20 us -> 0.65 us
  waiting for transfers between devices: 10.4 us -> 0 us
    dot_general x38 -> x0, matrix products: 54.3 us -> none  [the longest x3 7.55 us: backward_block(): jnp.einsum('the,she->hts', grad_block, v_block, preferred_element_type=jn...]
    pallas_call x0 -> x1, Pallas kernels: none -> 53.1 us  [body(): pl.pallas_call(functools.partial(kernel, nctx, ndp, heads, blocks, full_w...]
    another operation x4 -> x0, loops' own time: 48.1 us -> none  [the longest x1 25.8 us: prefix(): return lax.fori_loop(0, size, step, start)]
    psum x2 -> x0, blocking collectives: 42.4 us -> none  [the longest x1 39.9 us: body(): grad_gain = lax.psum(jnp.sum(cotangent * normed, axis=0), ('context', 'dp'))]
    ppermute x6 -> x0, starting transfers between devices: 24.2 us -> none  [shifted(): return lax.ppermute(block, axis, route)]
    dynamic_slice x31 -> x0, local copies, waits for them, and re-layouts: 23.1 us -> none  [the longest x24 20.9 us: body(): lax.scan(forward_block, (state_in, first_seg), (block_q, block_k, block_v...]
    slice x20 -> x0, local copies, waits for them, and re-layouts: 12.3 us -> none  [the longest x4 2.45 us: join_backward(): last_seg = jnp.where(high_segs[1] == 0.0, low_segs[1], high_segs[1])]
    all_gather x1 -> x0, blocking collectives: 12 us -> none  [prefix(): everything = jax.tree.map(lambda part: lax.all_gather(part, axis), value)]
  transfers between devices with their start and end apart: 7 -> 0, of which waited for: 3 -> 0; matrix products, arithmetic and copies ran while one was open for 4% -> 0% of each run, Pallas kernels for 0% -> 0%
where the time goes in v1:
time: 62.5 us; the launch traced here: 62.3 us
  Pallas kernels  53.1 us (85%)
  local copies, waits for them, and re-layouts  8.48 us (14%)
  between operations  0.65 us (1%)
    pallas_call x1, Pallas kernels, body(): pl.pallas_call(functools.partial(kernel, nctx, ndp, heads, blocks, full_w...  53.1 us
    unnamed x13, local copies, waits for them, and re-layouts  8.48 us

profile of v1, /device:TPU:0, one launch (start us, length us, event | category | flops | bytes accessed | tf_op | source)
XLA Modules:
  0.0 62.3 jit_solution(18260676795258214586)
XLA Ops:
  0.6 53.1 %shard_map.101 = (bf16[1,768,1024]{2,1,0:T(8,128)(2,1)}, bf16[1,768,1024]{2,1,0:T(8,128)(2,1)}, bf16[1,768,1024]{2,1,0:T(8,128)(2,1)}, bf16[1,768,1024]{2,1,0:T(8,128)(2,1)}, f32[8,128]{1,0:T(8,128)}) custom-call(s32[1,12]{1,0:T(1,128)} %seg_ref.1, f32[8,128]{1,0:T(8,128)} %bitcast.3, bf16[1,768,1024]{2,1,0:T(8,128)(2,1)} %q_hbm.1, ...), custom_call_target="tpu_custom_call" | custom-call | tf_op jit(solution)/shard_map/pallas_call | solution.py:386
  53.8 0.0 copy-start.2
  53.8 2.8 %copy.16 = bf16[1,768,1024]{2,1,0:T(8,128)(2,1)} copy(bf16[1,768,1024]{2,1,0:T(8,128)(2,1)} %get-tuple-element.20) | data formatting | bytes 3145728
  56.6 0.0 copy-done.2
  56.6 0.0 copy-start.1
  56.6 1.1 %copy.17 = bf16[1,768,1024]{2,1,0:T(8,128)(2,1)} copy(bf16[1,768,1024]{2,1,0:T(8,128)(2,1)S(1)} %copy-done.2) | data formatting | bytes 3145728
  57.7 0.8 %copy-done.1 = bf16[1,768,1024]{2,1,0:T(8,128)(2,1)S(1)} copy-done((bf16[1,768,1024]{2,1,0:T(8,128)(2,1)S(1)}, bf16[1,768,1024]{2,1,0:T(8,128)(2,1)}, u32[]{:S(2)}) %copy-start.1) | copy-done | bytes 1572888
  58.5 0.0 copy-start
  58.5 1.1 %copy.18 = bf16[1,768,1024]{2,1,0:T(8,128)(2,1)} copy(bf16[1,768,1024]{2,1,0:T(8,128)(2,1)S(1)} %copy-done.1) | data formatting | bytes 3145728
  59.7 0.8 %copy-done = bf16[1,768,1024]{2,1,0:T(8,128)(2,1)S(1)} copy-done((bf16[1,768,1024]{2,1,0:T(8,128)(2,1)S(1)}, bf16[1,768,1024]{2,1,0:T(8,128)(2,1)}, u32[]{:S(2)}) %copy-start) | copy-done | bytes 1572888
  60.5 0.0 copy-start.3
  60.5 1.1 %copy.19 = bf16[1,768,1024]{2,1,0:T(8,128)(2,1)} copy(bf16[1,768,1024]{2,1,0:T(8,128)(2,1)S(1)} %copy-done) | data formatting | bytes 3145728
  61.7 0.0 copy-done.3
  61.7 0.6 copy.20
Async XLA Ops:
  53.8 2.8 %copy-start.2 = (bf16[1,768,1024]{2,1,0:T(8,128)(2,1)S(1)}, bf16[1,768,1024]{2,1,0:T(8,128)(2,1)}, u32[]{:S(2)}) copy-start(bf16[1,768,1024]{2,1,0:T(8,128)(2,1)} %get-tuple-element.21) | copy-start | bytes 4718596
  56.6 2.0 %copy-start.1 = (bf16[1,768,1024]{2,1,0:T(8,128)(2,1)S(1)}, bf16[1,768,1024]{2,1,0:T(8,128)(2,1)}, u32[]{:S(2)}) copy-start(bf16[1,768,1024]{2,1,0:T(8,128)(2,1)} %get-tuple-element.22) | copy-start | bytes 4718596
  58.5 2.0 %copy-start = (bf16[1,768,1024]{2,1,0:T(8,128)(2,1)S(1)}, bf16[1,768,1024]{2,1,0:T(8,128)(2,1)}, u32[]{:S(2)}) copy-start(bf16[1,768,1024]{2,1,0:T(8,128)(2,1)} %get-tuple-element.23) | copy-start | bytes 4718596
  60.5 1.1 %copy-start.3 = (f32[8,128]{1,0:T(8,128)S(1)}, f32[8,128]{1,0:T(8,128)}, u32[]{:S(2)}) copy-start(f32[8,128]{1,0:T(8,128)} %get-tuple-element.14) | copy-start | bytes 12292

commit v2 on v1

v2 whole, which is shorter than its diff:
```python
import functools

import jax
import jax.numpy as jnp
from jax import lax
from jax.experimental import pallas as pl
from jax.experimental.pallas import tpu as pltpu
from jax.sharding import PartitionSpec as P

HD = 128
BLK = 256
SEGB = 64
PER = BLK // SEGB
LAG_F = 2
LAG_B = 3
F32 = jnp.float32
BF16 = jnp.bfloat16
MESH = pl.DeviceIdType.MESH


def nn(a, b):
    return lax.dot_general(a, b, (((1,), (0,)), ((), ())), preferred_element_type=F32)


def nt(a, b):
    return lax.dot_general(a, b, (((1,), (1,)), ((), ())), preferred_element_type=F32)


def tn(a, b):
    return lax.dot_general(a, b, (((0,), (0,)), ((), ())), preferred_element_type=F32)


def flag(cond):
    return jnp.where(cond, 1.0, 0.0).astype(F32)


def spread(index, ids):
    out = jnp.full(index.shape, ids[-1], jnp.int32)
    for i in reversed(range(len(ids) - 1)):
        out = jnp.where(index < (i + 1) * SEGB, ids[i], out)
    return out


def kernel(
    nctx, ndp, heads, blocks, width,
    seg_ref, gain_ref, q_hbm, k_hbm, v_hbm, g_hbm,
    no_s, gq_s, gk_s, gv_s, gg_ref,
    qs, ks, vs, gs,
    att, gv_part, weights, visible, mprev, mlast,
    local, state_bf, s_in, s_out, grad_local, g_in, g_out,
    sq_acc, in_acc, tile_out, tile_in, sums_out, sums_in,
    gg_part, gg_dp, gg_ctx_out, gg_ctx, datt, match_ref,
    in_sem, fs_sem, fr_sem, bs_sem, br_sem, ts_sem, tr_sem,
    xs_sem, xr_sem, ds_sem, dr_sem, cs_sem, cr_sem,
):
    ctx = lax.axis_index("context")
    ten = lax.axis_index("tensor")
    dp = lax.axis_index("dp")
    toks = blocks * BLK
    last = nctx - 1

    def in_copy(n, src, dst, h):
        cols = pl.ds(pl.multiple_of(h * HD, HD), HD)
        return pltpu.make_async_copy(src.at[0, :, cols], dst.at[h], in_sem.at[n, h])

    ins = ((k_hbm, ks), (v_hbm, vs), (q_hbm, qs), (g_hbm, gs))

    @pl.loop(0, heads)
    def _(h):
        for n in (0, 1):
            in_copy(n, *ins[n], h).start()

    @pl.loop(0, heads)
    def _(h):
        for n in (2, 3):
            in_copy(n, *ins[n], h).start()

    barrier = pltpu.get_barrier_semaphore()
    pl.semaphore_signal(barrier, inc=1, device_id={"tensor": 1 - ten}, device_id_type=MESH)

    @pl.loop(1, ndp)
    def _(d):
        pl.semaphore_signal(
            barrier, inc=1, device_id={"dp": lax.rem(dp + d, ndp)}, device_id_type=MESH
        )

    @pl.loop(1, nctx)
    def _(d):
        pl.semaphore_signal(
            barrier, inc=1, device_id={"context": lax.rem(ctx + d, nctx)}, device_id_type=MESH
        )

    seg = [[seg_ref[0, j * PER + i] for i in range(PER)] for j in range(blocks)]
    lasts = [seg[j][-1] for j in range(blocks)]
    tile_out[...] = jnp.full((8, HD), lasts[-1], jnp.int32).astype(F32)
    rows = lax.broadcasted_iota(jnp.int32, (BLK, BLK), 0)
    cols = lax.broadcasted_iota(jnp.int32, (BLK, BLK), 1)
    rows_h = lax.broadcasted_iota(jnp.int32, (BLK, HD), 0)
    for j in range(blocks):
        same = spread(rows, seg[j]) == spread(cols, seg[j])
        visible[j] = flag(jnp.logical_and(rows >= cols, same))
        seg_h = spread(rows_h, seg[j])
        at = pl.ds(j * BLK, BLK)
        mlast[at, :] = flag(seg_h == lasts[j]).astype(BF16)
        before = seg[0][0] if j == 0 else lasts[j - 1]
        mprev[at, :] = flag(seg_h == before).astype(BF16)
    step = [flag(seg[0][0] == lasts[0])]
    for j in range(1, blocks):
        step.append(flag(lasts[j - 1] == lasts[j]))

    pl.semaphore_wait(barrier, 1 + (ndp - 1) + (nctx - 1))

    def tile_copy():
        return pltpu.make_async_remote_copy(
            tile_out, tile_in, ts_sem, tr_sem,
            device_id={"context": jnp.minimum(ctx + 1, last)}, device_id_type=MESH,
        )

    def fwd_copy(h):
        return pltpu.make_async_remote_copy(
            s_out.at[h], s_in.at[h], fs_sem.at[h], fr_sem.at[h],
            device_id={"context": jnp.minimum(ctx + 1, last)}, device_id_type=MESH,
        )

    def bwd_copy(h):
        return pltpu.make_async_remote_copy(
            g_out.at[h], g_in.at[h], bs_sem.at[h], br_sem.at[h],
            device_id={"context": jnp.maximum(ctx - 1, 0)}, device_id_type=MESH,
        )

    @pl.when(ctx < last)
    def _():
        tile_copy().start()

    @pl.when(ctx == 0)
    def _():
        s_in[...] = jnp.zeros_like(s_in)
        tile_in[...] = jnp.full((8, HD), -1.0, F32)

    @pl.when(ctx == last)
    def _():
        g_in[...] = jnp.zeros_like(g_in)

    def rows_of(j):
        return pl.ds(j * BLK, BLK)

    sq_acc[...] = jnp.zeros_like(sq_acc)
    in_acc[...] = jnp.zeros_like(in_acc)

    @pl.loop(0, heads + LAG_F)
    def _(i):
        @pl.when(i == LAG_F)
        def _():
            @pl.when(ctx > 0)
            def _():
                tile_copy().wait_recv()

            first = jnp.full((1, HD), seg[0][0], jnp.int32).astype(F32)
            same = flag(tile_in[0:1, :] == first)
            match_ref[...] = jnp.broadcast_to(same, (8, HD))
            at = rows_of(0)
            mprev[at, :] = (mprev[at, :].astype(F32) * same).astype(BF16)

        @pl.when(i >= LAG_F)
        def _():
            h = i - LAG_F
            match = match_ref[0:1, :]
            reach = [match * step[0]]
            for j in range(1, blocks):
                reach.append(reach[-1] * step[j])

            @pl.when(ctx > 0)
            def _():
                fwd_copy(h).wait_recv()

            @pl.when(jnp.logical_and(ctx > 0, ctx < last))
            def _():
                s_out[h] = local[h, blocks - 1] + s_in[h] * reach[-1]
                fwd_copy(h).start()

            in_copy(3, *ins[3], h).wait()
            gain = gain_ref[pl.ds(h, 1), :]
            for j in range(blocks):
                at = rows_of(j)
                came = s_in[h]
                state = came if j == 0 else local[h, j - 1] + came * reach[j - 1]
                state = state.astype(BF16)
                state_bf[h, j] = state
                a = att[h, at, :] + nn(qs[h, at, :] * mprev[at, :], state)
                att[h, at, :] = a
                sq_acc[at, :] += a * a
                in_acc[at, :] += a * (gs[h, at, :].astype(F32) * gain)

        @pl.when(i < heads)
        def _():
            h = i
            for n in (0, 1):
                in_copy(n, *ins[n], h).wait()
            run = None
            for j in range(blocks):
                km = ks[h, rows_of(j), :] * mlast[rows_of(j), :]
                add = tn(km, vs[h, rows_of(j), :])
                run = add if run is None else run * step[j] + add
                local[h, j] = run

            @pl.when(jnp.logical_and(ctx == 0, ctx < last))
            def _():
                s_out[h] = local[h, blocks - 1]
                fwd_copy(h).start()

            in_copy(2, *ins[2], h).wait()
            for j in range(blocks):
                at = rows_of(j)
                w = (nt(qs[h, at, :], ks[h, at, :]) * visible[j]).astype(BF16)
                weights[h, j] = w
                att[h, at, :] = nn(w, vs[h, at, :])

    groups = toks // HD
    eye = (
        lax.broadcasted_iota(jnp.int32, (HD, HD), 0) == lax.broadcasted_iota(jnp.int32, (HD, HD), 1)
    )
    for n, acc in ((0, sq_acc), (1, in_acc)):
        for i in range(groups):
            col = jnp.sum(acc[pl.ds(i * HD, HD), :], axis=1, keepdims=True)
            row = jnp.sum(
                jnp.where(eye, jnp.broadcast_to(col, (HD, HD)), 0.0), axis=0, keepdims=True
            )
            sums_out[n, pl.ds(i, 1), :] = row
    swap = pltpu.make_async_remote_copy(
        sums_out, sums_in, xs_sem, xr_sem, device_id={"tensor": 1 - ten}, device_id_type=MESH
    )
    swap.start()
    swap.wait()
    total_sq = sums_out[0] + sums_in[0]
    total_in = sums_out[1] + sums_in[1]
    radius = jnp.sqrt(total_sq / width + 1e-06)
    inv = 1.0 / radius
    sums_out[0] = inv
    sums_out[1] = total_in / (width * radius * radius) * inv
    for n, acc in ((0, sq_acc), (1, in_acc)):
        for i in range(groups):
            row = jnp.broadcast_to(sums_out[n, pl.ds(i, 1), :], (HD, HD))
            acc[pl.ds(i * HD, HD), :] = row.T

    def dp_copy(to, slot):
        return pltpu.make_async_remote_copy(
            gg_part, gg_dp.at[slot], ds_sem.at[to], dr_sem.at[slot],
            device_id={"dp": to}, device_id_type=MESH,
        )

    def ctx_copy(to, slot):
        return pltpu.make_async_remote_copy(
            gg_ctx_out, gg_ctx.at[slot], cs_sem.at[to], cr_sem.at[slot],
            device_id={"context": to}, device_id_type=MESH,
        )

    match = match_ref[0:1, :]
    keep = [match * step[0]] + step[1:]
    full = [None] * (blocks + 1)
    full[blocks] = 1.0
    for j in reversed(range(blocks)):
        full[j] = full[j + 1] * keep[j]

    @pl.loop(0, heads + LAG_B)
    def _(i):
        @pl.when(i == heads)
        def _():
            gg_dp[dp] = gg_part[...]

            @pl.loop(1, ndp)
            def _(d):
                dp_copy(lax.rem(dp + d, ndp), dp).start()

        @pl.when(i >= LAG_B)
        def _():
            h = i - LAG_B

            @pl.when(ctx < last)
            def _():
                bwd_copy(h).wait_recv()

            @pl.when(jnp.logical_and(ctx < last, ctx > 0))
            def _():
                g_out[h] = grad_local[h, 0] + g_in[h] * full[0]
                bwd_copy(h).start()

            came = g_in[h]
            for j in range(blocks):
                at = rows_of(j)
                grad = came if j == blocks - 1 else grad_local[h, j + 1] + came * full[j + 1]
                grad = grad.astype(BF16)
                ml = mlast[at, :]
                gk_s[h, at, :] = (att[h, at, :] + nt(vs[h, at, :] * ml, grad)).astype(BF16)
                gv_s[h, at, :] = (gv_part[h, at, :] + nn(ks[h, at, :] * ml, grad)).astype(BF16)

        @pl.when(i == heads + 1)
        def _():
            @pl.loop(1, ndp)
            def _(d):
                peer = lax.rem(dp + d, ndp)
                dp_copy(peer, peer).wait_recv()

            part = gg_dp[0]
            for n in range(1, ndp):
                part = part + gg_dp[n]
            gg_ctx_out[...] = part
            gg_ctx[ctx] = part

            @pl.loop(1, nctx)
            def _(d):
                ctx_copy(lax.rem(ctx + d, nctx), ctx).start()

        @pl.when(i < heads)
        def _():
            h = i
            gain = gain_ref[pl.ds(h, 1), :]
            total = jnp.zeros((1, HD), F32)
            adds = []
            for j in range(blocks):
                at = rows_of(j)
                inv = sq_acc[at, :]
                a = att[h, at, :]
                g = gs[h, at, :].astype(F32)
                normed = a * inv
                no_s[h, at, :] = (normed * gain).astype(BF16)
                total = total + jnp.sum(g * normed, axis=0, keepdims=True)
                d = (g * gain * inv - a * in_acc[at, :]).astype(BF16)
                datt[at, :] = d
                adds.append(tn(qs[h, at, :] * mprev[at, :], d))
            gg_part[pl.ds(h, 1), :] = total
            run = None
            for j in reversed(range(blocks)):
                run = adds[j] if run is None else adds[j] + run * keep[j]
                grad_local[h, j] = run

            @pl.when(jnp.logical_and(ctx == last, ctx > 0))
            def _():
                g_out[h] = grad_local[h, 0]
                bwd_copy(h).start()

            for j in range(blocks):
                at = rows_of(j)
                d = datt[at, :]
                dw = (nt(d, vs[h, at, :]) * visible[j]).astype(BF16)
                gq = nn(dw, ks[h, at, :]) + nt(d * mprev[at, :], state_bf[h, j])
                gq_s[h, at, :] = gq.astype(BF16)
                att[h, at, :] = tn(dw, qs[h, at, :])
                gv_part[h, at, :] = tn(weights[h, j], d)

    @pl.loop(1, nctx)
    def _(d):
        peer = lax.rem(ctx + d, nctx)
        ctx_copy(peer, peer).wait()

    gg_ref[...] = lax.fori_loop(
        1, nctx, lambda i, total: total + gg_ctx[i], gg_ctx[0]
    )

    @pl.loop(1, ndp)
    def _(d):
        peer = lax.rem(dp + d, ndp)
        dp_copy(peer, peer).wait_send()

    @pl.when(ctx < last)
    def _():
        tile_copy().wait_send()

        @pl.loop(0, heads)
        def _(h):
            fwd_copy(h).wait_send()

    @pl.when(ctx > 0)
    def _():
        @pl.loop(0, heads)
        def _(h):
            bwd_copy(h).wait_send()


def writer(heads, *refs):
    sems, gain_sem = refs[10:]
    small = pltpu.make_async_copy(refs[4], refs[9], gain_sem)
    small.start()

    def copy(n, h):
        cols = pl.ds(pl.multiple_of(h * HD, HD), HD)
        return pltpu.make_async_copy(refs[n].at[h], refs[5 + n].at[0, :, cols], sems.at[n, h])

    @pl.loop(0, heads)
    def _(h):
        for n in range(4):
            copy(n, h).start()

    @pl.loop(0, heads)
    def _(h):
        for n in range(4):
            copy(n, h).wait()

    small.wait()


def body(nctx, ndp, full_width, queries, keys_in, values, norm_gain, segment_ids, grad_out):
    toks, local_width = queries.shape[1:]
    heads = local_width // HD
    blocks = toks // BLK
    wide = jax.ShapeDtypeStruct(queries.shape, BF16)
    hbm = pl.BlockSpec(memory_space=pl.ANY)
    vmem = pl.BlockSpec(memory_space=pltpu.VMEM)
    per_head = pltpu.VMEM((heads, toks, HD), BF16)
    states = pltpu.VMEM((heads, blocks, HD, HD), F32)
    hops = pltpu.VMEM((heads, HD, HD), F32)
    rowish = pltpu.VMEM((toks, HD), F32)
    dma = pltpu.SemaphoreType.DMA
    groups = -(-(toks // HD) // 8) * 8
    sums = pltpu.VMEM((2, groups, HD), F32)
    part = pltpu.VMEM((heads, HD), F32)
    outs = pl.pallas_call(
        functools.partial(kernel, nctx, ndp, heads, blocks, full_width),
        out_shape=[pltpu.VMEM((heads, toks, HD), BF16)] * 4 + [pltpu.VMEM((heads, HD), F32)],
        in_specs=[pl.BlockSpec(memory_space=pltpu.SMEM), vmem] + [hbm] * 4,
        out_specs=[vmem] * 4 + [vmem],
        scratch_shapes=[per_head] * 4
        + [
            pltpu.VMEM((heads, toks, HD), F32),
            pltpu.VMEM((heads, toks, HD), F32),
            pltpu.VMEM((heads, blocks, BLK, BLK), BF16),
            pltpu.VMEM((blocks, BLK, BLK), F32),
            pltpu.VMEM((toks, HD), BF16),
            pltpu.VMEM((toks, HD), BF16),
            states,
            pltpu.VMEM((heads, blocks, HD, HD), BF16),
            hops, hops, states, hops, hops,
            rowish, rowish,
            pltpu.VMEM((8, HD), F32), pltpu.VMEM((8, HD), F32),
            sums, sums,
            part,
            pltpu.VMEM((ndp, heads, HD), F32),
            part,
            pltpu.VMEM((nctx, heads, HD), F32),
            pltpu.VMEM((toks, HD), BF16),
            pltpu.VMEM((8, HD), F32),
            dma((4, heads)),
            dma((heads,)), dma((heads,)), dma((heads,)), dma((heads,)),
            dma, dma, dma, dma,
            dma((ndp,)), dma((ndp,)), dma((nctx,)), dma((nctx,)),
        ],
        compiler_params=pltpu.CompilerParams(
            collective_id=0, has_side_effects=True, vmem_limit_bytes=55 << 20
        ),
    )(segment_ids, norm_gain.reshape(heads, HD), queries, keys_in, values, grad_out)
    copies = pl.pallas_call(
        functools.partial(writer, heads),
        out_shape=[wide] * 4 + [jax.ShapeDtypeStruct((heads, HD), F32)],
        in_specs=[hbm] * 5,
        out_specs=[hbm] * 5,
        scratch_shapes=[dma((4, heads)), dma],
        compiler_params=pltpu.CompilerParams(vmem_limit_bytes=1 << 20),
    )(*outs)
    return (*copies[:4], copies[4].reshape(local_width))


def solution(mesh):
    wide = P("dp", "context", "tensor")
    in_specs = (wide, wide, wide, P("tensor"), P("dp", "context"), wide)
    out_specs = (wide, wide, wide, wide, P("tensor"))

    def run(queries, *rest):
        fn = functools.partial(
            body, mesh.shape["context"], mesh.shape["dp"], queries.shape[2]
        )
        return jax.shard_map(
            fn, mesh=mesh, in_specs=in_specs, out_specs=out_specs, check_vma=False
        )(queries, *rest)

    return run
```

time: 62.5 us -> 57.6 us (0.922)
  local copies, waits for them, and re-layouts: 8.48 us -> 0 us
  Pallas kernels: 53.1 us -> 56.7 us
    unnamed x13 -> x0, local copies, waits for them, and re-layouts: 8.48 us -> none
    pallas_call x0 -> x1, Pallas kernels: none -> 2.92 us  [body(): pl.pallas_call(functools.partial(writer, heads), out_shape=[wide] * 4 + [...]
    pallas_call x1, Pallas kernels: 53.1 us -> 53.8 us  [body(): pl.pallas_call(functools.partial(kernel, nctx, ndp, heads, blocks, full_w...]
where the time goes in v2:
time: 57.6 us; the launch traced here: 57.4 us
  Pallas kernels  56.7 us (98%)
  between operations  0.64 us (1%)
    pallas_call x1, Pallas kernels, body(): pl.pallas_call(functools.partial(kernel, nctx, ndp, heads, blocks, full_w...  53.8 us
    pallas_call x1, Pallas kernels, body(): pl.pallas_call(functools.partial(writer, heads), out_shape=[wide] * 4 + [...  2.92 us

profile of v2, /device:TPU:0, one launch (start us, length us, event | category | flops | bytes accessed | tf_op | source)
XLA Modules:
  0.0 57.4 jit_solution(208560072809159050)
XLA Ops:
  0.6 53.8 %shard_map.101 = (bf16[8,768,128]{2,1,0:T(8,128)(2,1)S(1)}, bf16[8,768,128]{2,1,0:T(8,128)(2,1)S(1)}, bf16[8,768,128]{2,1,0:T(8,128)(2,1)S(1)}, bf16[8,768,128]{2,1,0:T(8,128)(2,1)S(1)}, f32[8,128]{1,0:T(8,128)S(1)}) custom-call(s32[1,12]{1,0:T(1,128)} %seg_ref.1, f32[8,128]{1,0:T(8,128)} %bitcast.2, bf16[1,768,1024]{2,1,0:T(8,128)(2,1)} %q_hbm.1, ...), custom_call_target="tpu_custom_call" | custom-call | tf_op jit(solution)/shard_map/pallas_call | solution.py:416
  54.4 2.9 %shard_map.102 = (bf16[1,768,1024]{2,1,0:T(8,128)(2,1)}, bf16[1,768,1024]{2,1,0:T(8,128)(2,1)}, bf16[1,768,1024]{2,1,0:T(8,128)(2,1)}, bf16[1,768,1024]{2,1,0:T(8,128)(2,1)}, f32[8,128]{1,0:T(8,128)}) custom-call(bf16[8,768,128]{2,1,0:T(8,128)(2,1)S(1)} %get-tuple-element.15.refs_0_, bf16[8,768,128]{2,1,0:T(8,128)(2,1)S(1)} %get-tuple-element.16.refs_1_, ...), custom_call_target="tpu_custom_call" | custom-call | tf_op jit(solution)/shard_map/pallas_call | solution.py:450

commit v3 on v2

--- a/solution.py
+++ b/solution.py
@@ -11,8 +11,6 @@
 BLK = 256
 SEGB = 64
 PER = BLK // SEGB
-LAG_F = 2
-LAG_B = 3
 F32 = jnp.float32
 BF16 = jnp.bfloat16
 MESH = pl.DeviceIdType.MESH
@@ -46,7 +44,7 @@
     seg_ref, gain_ref, q_hbm, k_hbm, v_hbm, g_hbm,
     no_s, gq_s, gk_s, gv_s, gg_ref,
     qs, ks, vs, gs,
-    att, gv_part, weights, visible, mprev, mlast,
+    att, gv_part, weights_t, visible, visible_t, mprev, mlast,
     local, state_bf, s_in, s_out, grad_local, g_in, g_out,
     sq_acc, in_acc, tile_out, tile_in, sums_out, sums_in,
     gg_part, gg_dp, gg_ctx_out, gg_ctx, datt, match_ref,
@@ -58,12 +56,29 @@
     dp = lax.axis_index("dp")
     toks = blocks * BLK
     last = nctx - 1
+    lag_f = jnp.clip(3 * ctx, 2, heads)
+    lag_b = jnp.clip(2 * (last - ctx), 2, heads)
 
     def in_copy(n, src, dst, h):
         cols = pl.ds(pl.multiple_of(h * HD, HD), HD)
         return pltpu.make_async_copy(src.at[0, :, cols], dst.at[h], in_sem.at[n, h])
 
     ins = ((k_hbm, ks), (v_hbm, vs), (q_hbm, qs), (g_hbm, gs))
+
+    barrier = pltpu.get_barrier_semaphore()
+    pl.semaphore_signal(barrier, inc=1, device_id={"tensor": 1 - ten}, device_id_type=MESH)
+
+    @pl.loop(1, ndp)
+    def _(d):
+        pl.semaphore_signal(
+            barrier, inc=1, device_id={"dp": lax.rem(dp + d, ndp)}, device_id_type=MESH
+        )
+
+    @pl.loop(1, nctx)
+    def _(d):
+        pl.semaphore_signal(
+            barrier, inc=1, device_id={"context": lax.rem(ctx + d, nctx)}, device_id_type=MESH
+        )
 
     @pl.loop(0, heads)
     def _(h):
@@ -75,35 +90,13 @@
         for n in (2, 3):
             in_copy(n, *ins[n], h).start()
 
-    barrier = pltpu.get_barrier_semaphore()
-    pl.semaphore_signal(barrier, inc=1, device_id={"tensor": 1 - ten}, device_id_type=MESH)
-
-    @pl.loop(1, ndp)
-    def _(d):
-        pl.semaphore_signal(
-            barrier, inc=1, device_id={"dp": lax.rem(dp + d, ndp)}, device_id_type=MESH
-        )
-
-    @pl.loop(1, nctx)
-    def _(d):
-        pl.semaphore_signal(
-            barrier, inc=1, device_id={"context": lax.rem(ctx + d, nctx)}, device_id_type=MESH
-        )
-
     seg = [[seg_ref[0, j * PER + i] for i in range(PER)] for j in range(blocks)]
     lasts = [seg[j][-1] for j in range(blocks)]
     tile_out[...] = jnp.full((8, HD), lasts[-1], jnp.int32).astype(F32)
-    rows = lax.broadcasted_iota(jnp.int32, (BLK, BLK), 0)
-    cols = lax.broadcasted_iota(jnp.int32, (BLK, BLK), 1)
     rows_h = lax.broadcasted_iota(jnp.int32, (BLK, HD), 0)
     for j in range(blocks):
-        same = spread(rows, seg[j]) == spread(cols, seg[j])
-        visible[j] = flag(jnp.logical_and(rows >= cols, same))
         seg_h = spread(rows_h, seg[j])
-        at = pl.ds(j * BLK, BLK)
-        mlast[at, :] = flag(seg_h == lasts[j]).astype(BF16)
-        before = seg[0][0] if j == 0 else lasts[j - 1]
-        mprev[at, :] = flag(seg_h == before).astype(BF16)
+        mlast[pl.ds(j * BLK, BLK), :] = flag(seg_h == lasts[j]).astype(BF16)
     step = [flag(seg[0][0] == lasts[0])]
     for j in range(1, blocks):
         step.append(flag(lasts[j - 1] == lasts[j]))
@@ -144,12 +137,9 @@
     def rows_of(j):
         return pl.ds(j * BLK, BLK)
 
-    sq_acc[...] = jnp.zeros_like(sq_acc)
-    in_acc[...] = jnp.zeros_like(in_acc)
-
-    @pl.loop(0, heads + LAG_F)
+    @pl.loop(0, heads + lag_f)
     def _(i):
-        @pl.when(i == LAG_F)
+        @pl.when(i == lag_f)
         def _():
             @pl.when(ctx > 0)
             def _():
@@ -161,9 +151,9 @@
             at = rows_of(0)
             mprev[at, :] = (mprev[at, :].astype(F32) * same).astype(BF16)
 
-        @pl.when(i >= LAG_F)
-        def _():
-            h = i - LAG_F
+        @pl.when(i >= lag_f)
+        def _():
+            h = i - lag_f
             match = match_ref[0:1, :]
             reach = [match * step[0]]
             for j in range(1, blocks):
@@ -208,11 +198,25 @@
                 s_out[h] = local[h, blocks - 1]
                 fwd_copy(h).start()
 
+            @pl.when(i == 0)
+            def _():
+                rows = lax.broadcasted_iota(jnp.int32, (BLK, BLK), 0)
+                cols = lax.broadcasted_iota(jnp.int32, (BLK, BLK), 1)
+                for j in range(blocks):
+                    same = spread(rows, seg[j]) == spread(cols, seg[j])
+                    visible[j] = flag(jnp.logical_and(rows >= cols, same))
+                    visible_t[j] = flag(jnp.logical_and(cols >= rows, same))
+                    before = seg[0][0] if j == 0 else lasts[j - 1]
+                    mprev[rows_of(j), :] = flag(spread(rows_h, seg[j]) == before).astype(BF16)
+                sq_acc[...] = jnp.zeros_like(sq_acc)
+                in_acc[...] = jnp.zeros_like(in_acc)
+
             in_copy(2, *ins[2], h).wait()
             for j in range(blocks):
                 at = rows_of(j)
                 w = (nt(qs[h, at, :], ks[h, at, :]) * visible[j]).astype(BF16)
-                weights[h, j] = w
+                w_t = nt(ks[h, at, :], qs[h, at, :]) * visible_t[j]
+                weights_t[h, j] = w_t.astype(BF16)
                 att[h, at, :] = nn(w, vs[h, at, :])
 
     groups = toks // HD
@@ -261,7 +265,7 @@
     for j in reversed(range(blocks)):
         full[j] = full[j + 1] * keep[j]
 
-    @pl.loop(0, heads + LAG_B)
+    @pl.loop(0, heads + lag_b)
     def _(i):
         @pl.when(i == heads)
         def _():
@@ -271,9 +275,9 @@
             def _(d):
                 dp_copy(lax.rem(dp + d, ndp), dp).start()
 
-        @pl.when(i >= LAG_B)
-        def _():
-            h = i - LAG_B
+        @pl.when(i >= lag_b)
+        def _():
+            h = i - lag_b
 
             @pl.when(ctx < last)
             def _():
@@ -344,8 +348,9 @@
                 dw = (nt(d, vs[h, at, :]) * visible[j]).astype(BF16)
                 gq = nn(dw, ks[h, at, :]) + nt(d * mprev[at, :], state_bf[h, j])
                 gq_s[h, at, :] = gq.astype(BF16)
-                att[h, at, :] = tn(dw, qs[h, at, :])
-                gv_part[h, at, :] = tn(weights[h, j], d)
+                dw_t = (nt(vs[h, at, :], d) * visible_t[j]).astype(BF16)
+                att[h, at, :] = nn(dw_t, qs[h, at, :])
+                gv_part[h, at, :] = nn(weights_t[h, j], d)
 
     @pl.loop(1, nctx)
     def _(d):
@@ -423,6 +428,7 @@
             pltpu.VMEM((heads, toks, HD), F32),
             pltpu.VMEM((heads, toks, HD), F32),
             pltpu.VMEM((heads, blocks, BLK, BLK), BF16),
+            pltpu.VMEM((blocks, BLK, BLK), F32),
             pltpu.VMEM((blocks, BLK, BLK), F32),
             pltpu.VMEM((toks, HD), BF16),
             pltpu.VMEM((toks, HD), BF16),

time: 57.6 us -> 54.1 us (0.939)
  Pallas kernels: 56.7 us -> 53.3 us
    pallas_call x1, Pallas kernels: 53.8 us -> 50.4 us  [body(): pl.pallas_call(functools.partial(kernel, nctx, ndp, heads, blocks, full_w...]
where the time goes in v3:
time: 54.1 us; the launch traced here: 53.9 us
  Pallas kernels  53.3 us (99%)
  between operations  0.64 us (1%)
    pallas_call x1, Pallas kernels, body(): pl.pallas_call(functools.partial(kernel, nctx, ndp, heads, blocks, full_w...  50.4 us
    pallas_call x1, Pallas kernels, body(): pl.pallas_call(functools.partial(writer, heads), out_shape=[wide] * 4 + [...  2.92 us

profile of v3, /device:TPU:0, one launch (start us, length us, event | category | flops | bytes accessed | tf_op | source)
XLA Modules:
  0.0 53.9 jit_solution(7836664365488981144)
XLA Ops:
  0.6 50.4 %shard_map.101 = (bf16[8,768,128]{2,1,0:T(8,128)(2,1)S(1)}, bf16[8,768,128]{2,1,0:T(8,128)(2,1)S(1)}, bf16[8,768,128]{2,1,0:T(8,128)(2,1)S(1)}, bf16[8,768,128]{2,1,0:T(8,128)(2,1)S(1)}, f32[8,128]{1,0:T(8,128)S(1)}) custom-call(s32[1,12]{1,0:T(1,128)} %seg_ref.1, f32[8,128]{1,0:T(8,128)} %bitcast.2, bf16[1,768,1024]{2,1,0:T(8,128)(2,1)} %q_hbm.1, ...), custom_call_target="tpu_custom_call" | custom-call | tf_op jit(solution)/shard_map/pallas_call | solution.py:421
  51.0 2.9 %shard_map.102 = (bf16[1,768,1024]{2,1,0:T(8,128)(2,1)}, bf16[1,768,1024]{2,1,0:T(8,128)(2,1)}, bf16[1,768,1024]{2,1,0:T(8,128)(2,1)}, bf16[1,768,1024]{2,1,0:T(8,128)(2,1)}, f32[8,128]{1,0:T(8,128)}) custom-call(bf16[8,768,128]{2,1,0:T(8,128)(2,1)S(1)} %get-tuple-element.15.refs_0_, bf16[8,768,128]{2,1,0:T(8,128)(2,1)S(1)} %get-tuple-element.16.refs_1_, ...), custom_call_target="tpu_custom_call" | custom-call | tf_op jit(solution)/shard_map/pallas_call | solution.py:456
